TPU v7x, 512 devices: a whole 4x4x16 slice. The times are simulated.
512 devices in a mesh: tm: 64 (over y_hi, z, core), lat: 8 (over x, y_lo).
Axes of the slice: x: 4, y: 4 (y_hi: 2, y_lo: 2; y = y_hi * 2 + y_lo), z: 16, core: 2. Of those that a mesh axis runs over, the one named last changes fastest.
Arguments:
- fields: bfloat16 [128, 720, 1440], P('tm', 'lat'), may hold values from -6 to 6
- legendre: bfloat16 [720, 8192], P('lat'), may hold values from -0.21875 to 0.21875
- order_table: int32 [3, 16384], replicated, may hold values from 0 to 720, as said below
- window_start: int32 [1], replicated, may hold values from 0 to 8192
- ridge: float32 [1], replicated, may hold values from 0.3 to 1
Outputs:
- factored: float32 [8192, 8192], P('tm', 'lat')
Inputs may be any that keep to these rules, and one draw needn't show every extreme that they name: `order_table`: row 0 holds each entry's degree, row 1 its order, which is at most the degree and below 720, row 2 is 0 for a cosine and 1 for a sine part, and is 1 only where the order is positive.
All inputs are finite; a program needn't handle non-finite values.
Results may differ from a plain program's by a relative error of at most 0.0048.
Values may be sent and summed in bfloat16 or wider, within the bound.
A program may use at most 64 MiB of HBM per device.

v0:
```python
import math

import jax
import jax.numpy as jnp
from jax import lax
from jax.sharding import PartitionSpec as P

LMAX = 720
PANEL = 512


def split_up(shard, dim, devices):
    before, after = (shard.shape[:dim], shard.shape[dim + 1 :])
    return jnp.moveaxis(shard.reshape(*before, devices, -1, *after), dim, 0)


def sum_at_owner(shard, axis, dim):
    devices = lax.axis_size(axis)
    blocks = lax.all_to_all(split_up(shard, dim, devices), axis, 0, 0, tiled=True)
    return jnp.sum(blocks, axis=0)


def sent_to_all(shard, axis):
    copies = jnp.broadcast_to(shard, (lax.axis_size(axis), *shard.shape))
    return lax.all_to_all(copies, axis, split_axis=0, concat_axis=0, tiled=True)


def in_order(blocks, dim):
    blocks = jnp.moveaxis(blocks, 0, dim)
    shape = blocks.shape
    return blocks.reshape(*shape[:dim], shape[dim] * shape[dim + 1], *shape[dim + 2 :])


def gather_directly(shard, axis, dim):
    blocks = sent_to_all(shard, axis)
    return in_order(blocks, dim)


def from_root(shard, axis, root):
    return lax.dynamic_index_in_dim(lax.all_gather(shard, axis), root, 0, keepdims=False)


def make_basis(nlon):
    half = nlon // 2
    longitude = jnp.arange(nlon, dtype=jnp.int32)[:, None]
    column = jnp.arange(nlon, dtype=jnp.int32)[None, :]
    freq = column % half
    phase = (freq * longitude % nlon).astype(jnp.float32) * (2.0 * math.pi / nlon)
    return jnp.where(column < half, jnp.cos(phase), jnp.sin(phase)).astype(jnp.bfloat16)


def legendre_contract(spectra, legendre, column):
    kcoef = legendre.shape[1]
    width = kcoef // 8

    def one_part(number):
        start = number * width
        chosen_cols = lax.dynamic_slice_in_dim(column, start, width, 0)
        weights = lax.dynamic_slice_in_dim(legendre, start, width, 1).astype(jnp.float32)
        chosen = jnp.take(spectra, chosen_cols, axis=2)
        return jnp.einsum("tlk,lk->tk", chosen, weights)

    parts_out = lax.map(one_part, jnp.arange(8, dtype=jnp.int32))
    return jnp.transpose(parts_out, (1, 0, 2)).reshape(spectra.shape[0], kcoef)


def gram_dot(left, right):
    return lax.dot_general(
        left, right, (((0,), (0,)), ((), ())), preferred_element_type=jnp.float32
    )


def on_device(fields, legendre, order_table, window_start, ridge):
    times_dev, lat_dev, nlon = fields.shape
    kcoef = legendre.shape[1]
    tm_count = lax.axis_size("tm")
    lat_count = lax.axis_size("lat")
    rows_width = kcoef // tm_count
    cols_width = kcoef // lat_count
    tm_index = lax.axis_index("tm")
    lat_index = lax.axis_index("lat")
    window = lax.dynamic_slice_in_dim(order_table, window_start[0], kcoef, 1)
    degree = window[0]
    column = window[1] + nlon // 2 * window[2]
    ridge_diag = ridge[0] * (
        1.0 + (degree * (degree + 1)).astype(jnp.float32) / float(LMAX * (LMAX + 1))
    )
    dft_basis = make_basis(nlon)
    flat = fields.reshape(times_dev * lat_dev, nlon)
    spectra = (
        jnp.dot(flat, dft_basis, preferred_element_type=jnp.float32) * (1.0 / math.sqrt(nlon))
    ).reshape(times_dev, lat_dev, nlon)
    partial_value = legendre_contract(spectra, legendre, column)
    own_share = sum_at_owner(partial_value, "lat", 1).astype(jnp.bfloat16)
    col_block = gather_directly(own_share, "tm", 0)
    root_index = tm_index * rows_width // cols_width
    offset = jnp.clip(tm_index * rows_width - lat_index * cols_width, 0, cols_width - rows_width)
    row_piece = lax.dynamic_slice_in_dim(col_block, offset, rows_width, 1)
    row_block = from_root(row_piece, "lat", root_index)
    panel_coef = from_root(col_block[:, :PANEL], "lat", 0)
    inverse = 1.0 / col_block.shape[0]
    row_glob = tm_index * rows_width + jnp.arange(rows_width, dtype=jnp.int32)
    col_glob = lat_index * cols_width + jnp.arange(cols_width, dtype=jnp.int32)
    panel_pos = jnp.arange(PANEL, dtype=jnp.int32)
    ridge_rows = lax.dynamic_slice_in_dim(ridge_diag, tm_index * rows_width, rows_width, 0)
    zero = jnp.float32(0.0)
    gram_tile = gram_dot(row_block, col_block) * inverse + jnp.where(
        row_glob[:, None] == col_glob[None, :], ridge_rows[:, None], zero
    )
    panel_gram = gram_dot(panel_coef, panel_coef) * inverse + jnp.diag(ridge_diag[:PANEL])
    factor = jnp.linalg.cholesky(panel_gram)
    row_panel = gram_dot(row_block, panel_coef) * inverse + jnp.where(
        row_glob[:, None] == panel_pos[None, :], ridge_rows[:, None], zero
    )
    panel_rows = jax.scipy.linalg.solve_triangular(factor, row_panel.T, lower=True).T
    solved = jax.scipy.linalg.solve_triangular(factor, panel_coef.astype(jnp.float32).T, lower=True)
    upper = (
        jnp.dot(
            solved, col_block, precision=lax.Precision.HIGHEST, preferred_element_type=jnp.float32
        )
        * inverse
    )
    update = jnp.dot(panel_rows, upper, precision=lax.Precision.HIGHEST)
    upper_rows = lax.dynamic_slice_in_dim(
        upper, jnp.minimum(tm_index * rows_width, PANEL - rows_width), rows_width, 0
    )
    left_part = jnp.pad(panel_rows, ((0, 0), (0, cols_width - PANEL)))
    return jnp.where(
        col_glob[None, :] < PANEL,
        left_part,
        jnp.where(row_glob[:, None] < PANEL, upper_rows, gram_tile - update),
    )


def solution(mesh):
    placed = (P("tm", "lat", None), P("lat", None), P(), P(), P())
    return jax.shard_map(
        on_device, mesh=mesh, in_specs=placed, out_specs=P("tm", "lat"), check_vma=False
    )
```

profile of v0, /device:TPU:16, one launch (start us, length us, event | category | flops | bytes accessed | tf_op | source)
XLA Modules:
  0.0 470.9 jit_solution(15270033936218827151)
XLA Ops:
  7.2 1.1 copy.11
  8.6 37.4 %select_convert_fusion.8 = bf16[1440,1440]{1,0:T(8,128)(2,1)S(1)} fusion(s32[1440]{0:T(1024)S(1)} %add_select_fusion.1, pred[1440]{0:T(1024)(128)(4,1)S(1)} %iota_compare_fusion.6), kind=kLoop, calls=%fused_computation.13.clone.clone.clone.clone.clone.clone.1 | loop fusion | flops 22809600 | bytes 4154400 | tf_op jit(solution)/shard_map/dot_general | solution.py:91
  45.9 1.1 fusion.10
  47.1 2.1 copy.12
  49.2 1.3 constant_dynamic-slice_fusion.2
  50.5 176.4 %while.14 = (s32[]{:T(128)}, f32[8,2,1024]{2,1,0:T(2,128)S(1)}, s32[8]{0:T(128)S(1)}, bf16[90,8192]{1,0:T(8,128)(2,1)}, s32[8192]{0:T(1024)S(1)}, /*index=5*/f32...) while((s32[]{:T(128)}, f32[8,2,1024]{2,1,0:T(2,128)S(1)}, s32[8]{0:T(128)S(1)}, ...), condition=%wide.region_1.2_spmd, body=%wide.region_0.1_spmd.sunk | while | flops 653318 | bytes 3930287 | solution.py:63
  51.8 4.9 %gather_fusion = f32[1024,2,90]{2,1,0:T(2,128)S(1)} fusion(f32[2,90,1440]{1,0,2:T(2,128)} %get-tuple-element.190, s32[1024]{0:T(1024)S(1)} %fusion.110), kind=kCustom, calls=%fused_computation.clone.1 | custom fusion | bytes 1478656 | tf_op jit(solution)/shard_map/while/body/eval_jaxpr/jit(_take)/gather | solution.py:60
  56.8 1.0 bitcast_convert_fusion.2
  57.9 14.5 %fusion.111 = f32[1024,2]{1,0:T(8,128)S(1)} fusion(f32[1024,2,90]{2,1,0:T(2,128)S(1)} %gather_fusion, pred[1024]{0:T(1024)(128)(4,1)S(1)} %compare_and_fusion.2, f32[1024,90]{1,0:T(8,128)S(1)} %copy.30), kind=kLoop, calls=%fused_computation.4.clone.1 | loop fusion | flops 550912 | bytes 1115136 | tf_op jit(solution)/shard_map/while
  72.6 0.6 dynamic_slice.59
  73.9 4.9 %gather_fusion = f32[1024,2,90]{2,1,0:T(2,128)S(1)} fusion(f32[2,90,1440]{1,0,2:T(2,128)} %get-tuple-element.190, s32[1024]{0:T(1024)S(1)} %fusion.110), kind=kCustom, calls=%fused_computation.clone.1 | custom fusion | bytes 1478656 | tf_op jit(solution)/shard_map/while/body/eval_jaxpr/jit(_take)/gather | solution.py:60
  78.8 1.0 bitcast_convert_fusion.2
  80.0 14.5 %fusion.111 = f32[1024,2]{1,0:T(8,128)S(1)} fusion(f32[1024,2,90]{2,1,0:T(2,128)S(1)} %gather_fusion, pred[1024]{0:T(1024)(128)(4,1)S(1)} %compare_and_fusion.2, f32[1024,90]{1,0:T(8,128)S(1)} %copy.30), kind=kLoop, calls=%fused_computation.4.clone.1 | loop fusion | flops 550912 | bytes 1115136 | tf_op jit(solution)/shard_map/while
  94.7 0.6 dynamic_slice.59
  95.9 4.9 %gather_fusion = f32[1024,2,90]{2,1,0:T(2,128)S(1)} fusion(f32[2,90,1440]{1,0,2:T(2,128)} %get-tuple-element.190, s32[1024]{0:T(1024)S(1)} %fusion.110), kind=kCustom, calls=%fused_computation.clone.1 | custom fusion | bytes 1478656 | tf_op jit(solution)/shard_map/while/body/eval_jaxpr/jit(_take)/gather | solution.py:60
  100.9 1.0 bitcast_convert_fusion.2
  102.0 14.5 %fusion.111 = f32[1024,2]{1,0:T(8,128)S(1)} fusion(f32[1024,2,90]{2,1,0:T(2,128)S(1)} %gather_fusion, pred[1024]{0:T(1024)(128)(4,1)S(1)} %compare_and_fusion.2, f32[1024,90]{1,0:T(8,128)S(1)} %copy.30), kind=kLoop, calls=%fused_computation.4.clone.1 | loop fusion | flops 550912 | bytes 1115136 | tf_op jit(solution)/shard_map/while
  116.7 0.6 dynamic_slice.59
  118.0 4.9 %gather_fusion = f32[1024,2,90]{2,1,0:T(2,128)S(1)} fusion(f32[2,90,1440]{1,0,2:T(2,128)} %get-tuple-element.190, s32[1024]{0:T(1024)S(1)} %fusion.110), kind=kCustom, calls=%fused_computation.clone.1 | custom fusion | bytes 1478656 | tf_op jit(solution)/shard_map/while/body/eval_jaxpr/jit(_take)/gather | solution.py:60
  122.9 1.0 bitcast_convert_fusion.2
  124.1 14.5 %fusion.111 = f32[1024,2]{1,0:T(8,128)S(1)} fusion(f32[1024,2,90]{2,1,0:T(2,128)S(1)} %gather_fusion, pred[1024]{0:T(1024)(128)(4,1)S(1)} %compare_and_fusion.2, f32[1024,90]{1,0:T(8,128)S(1)} %copy.30), kind=kLoop, calls=%fused_computation.4.clone.1 | loop fusion | flops 550912 | bytes 1115136 | tf_op jit(solution)/shard_map/while
  138.8 0.6 dynamic_slice.59
  140.0 4.9 %gather_fusion = f32[1024,2,90]{2,1,0:T(2,128)S(1)} fusion(f32[2,90,1440]{1,0,2:T(2,128)} %get-tuple-element.190, s32[1024]{0:T(1024)S(1)} %fusion.110), kind=kCustom, calls=%fused_computation.clone.1 | custom fusion | bytes 1478656 | tf_op jit(solution)/shard_map/while/body/eval_jaxpr/jit(_take)/gather | solution.py:60
  145.0 1.0 bitcast_convert_fusion.2
  146.2 14.5 %fusion.111 = f32[1024,2]{1,0:T(8,128)S(1)} fusion(f32[1024,2,90]{2,1,0:T(2,128)S(1)} %gather_fusion, pred[1024]{0:T(1024)(128)(4,1)S(1)} %compare_and_fusion.2, f32[1024,90]{1,0:T(8,128)S(1)} %copy.30), kind=kLoop, calls=%fused_computation.4.clone.1 | loop fusion | flops 550912 | bytes 1115136 | tf_op jit(solution)/shard_map/while
  160.8 0.6 dynamic_slice.59
  162.1 4.9 %gather_fusion = f32[1024,2,90]{2,1,0:T(2,128)S(1)} fusion(f32[2,90,1440]{1,0,2:T(2,128)} %get-tuple-element.190, s32[1024]{0:T(1024)S(1)} %fusion.110), kind=kCustom, calls=%fused_computation.clone.1 | custom fusion | bytes 1478656 | tf_op jit(solution)/shard_map/while/body/eval_jaxpr/jit(_take)/gather | solution.py:60
  167.0 1.0 bitcast_convert_fusion.2
  168.2 14.5 %fusion.111 = f32[1024,2]{1,0:T(8,128)S(1)} fusion(f32[1024,2,90]{2,1,0:T(2,128)S(1)} %gather_fusion, pred[1024]{0:T(1024)(128)(4,1)S(1)} %compare_and_fusion.2, f32[1024,90]{1,0:T(8,128)S(1)} %copy.30), kind=kLoop, calls=%fused_computation.4.clone.1 | loop fusion | flops 550912 | bytes 1115136 | tf_op jit(solution)/shard_map/while
  184.1 4.9 %gather_fusion = f32[1024,2,90]{2,1,0:T(2,128)S(1)} fusion(f32[2,90,1440]{1,0,2:T(2,128)} %get-tuple-element.190, s32[1024]{0:T(1024)S(1)} %fusion.110), kind=kCustom, calls=%fused_computation.clone.1 | custom fusion | bytes 1478656 | tf_op jit(solution)/shard_map/while/body/eval_jaxpr/jit(_take)/gather | solution.py:60
  189.1 1.0 bitcast_convert_fusion.2
  190.3 14.5 %fusion.111 = f32[1024,2]{1,0:T(8,128)S(1)} fusion(f32[1024,2,90]{2,1,0:T(2,128)S(1)} %gather_fusion, pred[1024]{0:T(1024)(128)(4,1)S(1)} %compare_and_fusion.2, f32[1024,90]{1,0:T(8,128)S(1)} %copy.30), kind=kLoop, calls=%fused_computation.4.clone.1 | loop fusion | flops 550912 | bytes 1115136 | tf_op jit(solution)/shard_map/while
  206.2 4.9 %gather_fusion = f32[1024,2,90]{2,1,0:T(2,128)S(1)} fusion(f32[2,90,1440]{1,0,2:T(2,128)} %get-tuple-element.190, s32[1024]{0:T(1024)S(1)} %fusion.110), kind=kCustom, calls=%fused_computation.clone.1 | custom fusion | bytes 1478656 | tf_op jit(solution)/shard_map/while/body/eval_jaxpr/jit(_take)/gather | solution.py:60
  211.1 1.0 bitcast_convert_fusion.2
  212.3 14.5 %fusion.111 = f32[1024,2]{1,0:T(8,128)S(1)} fusion(f32[1024,2,90]{2,1,0:T(2,128)S(1)} %gather_fusion, pred[1024]{0:T(1024)(128)(4,1)S(1)} %compare_and_fusion.2, f32[1024,90]{1,0:T(8,128)S(1)} %copy.30), kind=kLoop, calls=%fused_computation.4.clone.1 | loop fusion | flops 550912 | bytes 1115136 | tf_op jit(solution)/shard_map/while
  227.0 11.1 %all_to_all.10 = f32[8,2,1024]{2,1,0:T(2,128)S(1)} all-to-all(f32[8,2,1024]{2,1,0:T(2,128)S(1)} %get-tuple-element.38), channel_id=1, replica_groups=mesh['tm'=64,'lat'=8] {'lat'}, dimensions={0} | all-to-all | bytes 131072 | tf_op jit(solution)/shard_map/all_to_all | solution.py:19
  238.2 38.5 %all_to_all.11 = bf16[64,2,1024]{2,1,0:T(2,128)(2,1)S(1)} all-to-all(bf16[64,2,1024]{2,1,0:T(2,128)(2,1)S(1)} %broadcast_in_dim.105), channel_id=1, replica_groups=mesh['tm'=64,'lat'=8] {'tm'}, dimensions={0} | all-to-all | bytes 524288 | tf_op jit(solution)/shard_map/all_to_all | solution.py:25
  276.9 0.7 slice.140
  278.5 29.0 %all-gather.1 = bf16[1024,128]{1,0:T(8,128)(2,1)S(1)} all-gather(bf16[128,128]{1,0:T(8,128)(2,1)S(1)} %constant_dynamic-slice_fusion.1), channel_id=3, replica_groups=mesh['tm'=64,'lat'=8] {'lat'}, dimensions={0}, use_global_device_ids=true | all-gather | bytes 294912 | tf_op jit(solution)/shard_map/all_gather | solution.py:40
  307.5 0.7 copy-done.1
  308.2 1.1 fusion.13
  309.3 7.9 %all-gather.4.cloned.1.call-done = bf16[1024,512]{1,0:T(8,128)(2,1)} async-done(((bf16[128,512]{1,0:T(8,128)(2,1)}), bf16[1024,512]{1,0:T(8,128)(2,1)}) %all-gather.4.cloned.1.call-update) | async-done | bytes 1048592 | tf_op jit(solution)/shard_map/all_gather | solution.py:40
  317.1 1.3 convolution_multiply_fusion.1
  319.0 11.7 %cholesky.103 = f32[128,128]{1,0:T(8,128)S(1)} custom-call(f32[128,128]{1,0:T(8,128)S(1)} %cholesky.263), custom_call_target="Cholesky" | custom-call | tf_op jit(solution)/shard_map/jit(cholesky)/cholesky | solution.py:111
  330.9 9.8 %custom-call.30 = f32[1,128,128]{1,2,0:T(8,128)S(1)} custom-call(f32[1,128,128]{2,1,0:T(8,128)S(1)} %get-tuple-element.94), custom_call_target="InvertDiagBlocksLowerTriangular" | custom-call | tf_op jit(solution)/shard_map/jit(cholesky)/cholesky | solution.py:111
  341.4 11.7 %cholesky.215 = f32[128,128]{1,0:T(8,128)S(1)} custom-call(f32[128,128]{1,0:T(8,128)S(1)} %cholesky.267), custom_call_target="Cholesky" | custom-call | tf_op jit(solution)/shard_map/jit(cholesky)/cholesky | solution.py:111
  353.2 10.0 %custom-call.31 = f32[1,128,128]{1,2,0:T(8,128)S(1)} custom-call(f32[1,128,128]{2,1,0:T(8,128)S(1)} %get-tuple-element.91), custom_call_target="InvertDiagBlocksLowerTriangular" | custom-call | tf_op jit(solution)/shard_map/jit(cholesky)/cholesky | solution.py:111
  363.8 11.7 %cholesky.236 = f32[128,128]{1,0:T(8,128)S(1)} custom-call(f32[128,128]{1,0:T(8,128)S(1)} %cholesky.272), custom_call_target="Cholesky" | custom-call | tf_op jit(solution)/shard_map/jit(cholesky)/cholesky | solution.py:111
  375.6 0.7 compare_reduce_fusion.1
  376.3 9.8 %custom-call.32 = f32[1,128,128]{1,2,0:T(8,128)S(1)} custom-call(f32[1,128,128]{2,1,0:T(8,128)S(1)} %get-tuple-element.88), custom_call_target="InvertDiagBlocksLowerTriangular" | custom-call | tf_op jit(solution)/shard_map/jit(cholesky)/cholesky | solution.py:111
  386.7 11.9 %cholesky.253 = f32[128,128]{1,0:T(8,128)S(1)} custom-call(f32[128,128]{1,0:T(8,128)S(1)} %convolution_subtract_fusion.9), custom_call_target="Cholesky" | custom-call | tf_op jit(solution)/shard_map/jit(cholesky)/cholesky | solution.py:111
  398.6 0.7 compare_reduce_fusion
  399.4 0.7 compare_reduce_fusion.2
  402.7 10.5 %while.15 = (s32[]{:T(128)}, f32[512,512]{1,0:T(8,128)S(1)}, s32[4,2]{0,1:T(2,128)S(1)}, f32[4,128,128]{2,1,0:T(8,128)}, s32[]{:T(128)}) while((s32[]{:T(128)}, f32[512,512]{1,0:T(8,128)S(1)}, s32[4,2]{0,1:T(2,128)S(1)}, f32[4,128,128]{2,1,0:T(8,128)}, s32[]{:T(128)}) %tuple.50), condition=%wide.while_cond, body=%wide.while_body.sunk | while | flops 2 | bytes 132705 | solution.py:115
  403.4 1.9 bitcast_dynamic-update-slice_fusion.5
  406.0 2.0 bitcast_dynamic-update-slice_fusion.5
  408.6 2.0 bitcast_dynamic-update-slice_fusion.5
  411.2 2.0 bitcast_dynamic-update-slice_fusion.5
  413.2 40.1 %custom-call.34 = f32[4,128,128]{1,2,0:T(8,128)S(1)} custom-call(f32[4,128,128]{2,1,0:T(8,128)} %get-tuple-element.53), custom_call_target="InvertDiagBlocksLowerTriangular" | custom-call | tf_op jit(solution)/shard_map/jit(_solve_triangular)/triangular_solve | solution.py:115
  453.3 1.1 fusion.14
  456.4 0.9 convert_bitcast_fusion
  459.7 1.0 convolution_multiply_fusion
  460.8 1.8 fusion.12
  462.6 1.0 copy.17
  (108 shorter events, 15.9 us)
Async XLA Ops:
  6.5 310.6 %all-gather.4.cloned.1.call-start = ((), (), s32[]{:S(2)}) async-start(), calls=%async_computation.2 | async-start | bytes 1179648 | tf_op jit(solution)/shard_map/all_gather | solution.py:40
  307.5 0.7 copy-start.1
  457.7 3.1 copy-start
Sparse Core Ops, SparseCore 0:
  277.7 39.4 all-gather.3
where the time goes:
time: 478 us; the launch traced here: 471 us
  other arithmetic  283 us (59%)
  blocking collectives  78.6 us (16%)
  local copies, waits for them, and re-layouts  64.6 us (14%)
  between operations  18.1 us (4%)
  matrix products  13.5 us (3%)
  waiting for transfers between devices  7.89 us (2%)
  loops' own time  5.37 us (1%)
    while x16, other arithmetic  123 us
    another operation x14, other arithmetic, on_device(): factor = jnp.linalg.cholesky(panel_gram)  78.9 us
    another operation x4, other arithmetic, on_device(): jax.scipy.linalg.solve_triangular(factor, row_panel.T, lower=True)  40.3 us
    gather x8, local copies, waits for them, and re-layouts, one_part(): chosen = jnp.take(spectra, chosen_cols, axis=2)  39.3 us
    all_to_all x1, blocking collectives, sent_to_all(): return lax.all_to_all(copies, axis, split_axis=0, concat_axis=0, tiled=True)  38.5 us
    dot_general x1, other arithmetic, on_device(): jnp.dot(flat, dft_basis, preferred_element_type=jnp.float32)  37.4 us
    all_gather x1, blocking collectives, from_root(): lax.all_gather(shard, axis)  29 us
    all_to_all x1, blocking collectives, sum_at_owner(): lax.all_to_all(split_up(shard, dim, devices), axis, 0, 0, tiled=True)  11.1 us
  transfers between devices with their start and end apart: 1, of which 1 were waited for; matrix products, arithmetic and copies ran while one was open for 0% of the time, Pallas kernels for 0%

commit v1 on v0

v1 whole, which is shorter than its diff:
```python
import math

import jax
import jax.numpy as jnp
import numpy as np
from jax import lax
from jax.experimental import pallas as pl
from jax.experimental.pallas import tpu as pltpu
from jax.sharding import PartitionSpec as P

NLON = 1440
HALF = NLON // 2
LMAX = 720
NT = 128
PANEL = 512
BLOCK = 128
WIDTH = 1024
SENT = WIDTH + PANEL
LAT = 90
LATPAD = 96
DEEP = 768
CHUNK = 256
F32 = jnp.float32
BF16 = jnp.bfloat16


def half_basis():
    n = np.arange(HALF)[:, None]
    c = np.arange(HALF)[None, :]
    phase = ((n * c) % NLON).astype(np.float32) * np.float32(2.0 * math.pi / NLON)
    basis = np.zeros((2, HALF, DEEP), np.float32)
    basis[0, :, :HALF] = np.cos(phase)
    basis[1, :, :HALF] = np.sin(phase)
    return basis.astype(BF16)


def spectral_kernel(fields_ref, basis_ref, leg_ref, win_ref, out_ref, rows):
    @pl.when(pl.program_id(0) == 0)
    def _():
        lane = lax.broadcasted_iota(jnp.int32, (1, DEEP), 1)
        sign = jnp.where(lane % 2 == 0, 1.0, -1.0).astype(F32)
        for t in range(2):
            low, high = fields_ref[t, :, :HALF], fields_ref[t, :, HALF:]
            for p in range(2):
                basis = basis_ref[p]
                first = jnp.dot(low, basis, preferred_element_type=F32)
                second = jnp.dot(high, basis, preferred_element_type=F32)
                at = (2 * p + t) * LATPAD
                rows[at : at + LAT, :] = (first + sign * second).astype(BF16)

    iota = lax.broadcasted_iota(jnp.int32, (CHUNK, CHUNK), 0).astype(F32).astype(BF16)
    one, zero = jnp.ones((CHUNK, CHUNK), BF16), jnp.zeros((CHUNK, CHUNK), BF16)
    for n in range(WIDTH // CHUNK):
        cols = slice(n * CHUNK, (n + 1) * CHUNK)
        order, part = win_ref[1:2, cols], win_ref[2:3, cols]
        picked = None
        for q in range(DEEP // CHUNK):
            rel = jnp.clip(order - CHUNK * q, -1, CHUNK).astype(F32).astype(BF16)
            onehot = jnp.where(iota == rel, one, zero)
            term = jnp.dot(
                rows[:, q * CHUNK : (q + 1) * CHUNK], onehot, preferred_element_type=F32
            )
            picked = term if picked is None else picked + term
        weights = leg_ref[:, cols].astype(F32)
        for t in range(2):
            cosine = picked[t * LATPAD : t * LATPAD + LAT]
            sine = picked[(2 + t) * LATPAD : (2 + t) * LATPAD + LAT]
            chosen = jnp.where(part > 0, sine, cosine)
            out_ref[0, t : t + 1, cols] = jnp.sum(chosen * weights, axis=0, keepdims=True)


def partial_coeffs(fields, legendre, window):
    kcoef = legendre.shape[1]
    return pl.pallas_call(
        spectral_kernel,
        grid=(kcoef // WIDTH,),
        in_specs=[
            pl.BlockSpec((2, LAT, NLON), lambda k: (0, 0, 0)),
            pl.BlockSpec((2, HALF, DEEP), lambda k: (0, 0, 0)),
            pl.BlockSpec((LAT, WIDTH), lambda k: (0, k)),
            pl.BlockSpec((3, WIDTH), lambda k: (0, k)),
        ],
        out_specs=pl.BlockSpec((1, 2, WIDTH), lambda k: (k, 0, 0)),
        out_shape=jax.ShapeDtypeStruct((kcoef // WIDTH, 2, WIDTH), F32),
        scratch_shapes=[pltpu.VMEM((4 * LATPAD, DEEP), BF16)],
        name="spectral",
    )(fields, jnp.asarray(half_basis()), legendre, window)


def exchange_kernel(
    part_ref, all_ref, row_ref, got, got1, own, far, send, rs, rs1, fs, ns, cs, ws, send2, keep
):
    i, j = lax.axis_index("tm"), lax.axis_index("lat")
    core, z, yh = i % 2, (i // 2) % 16, i // 32

    def tm_of(y_part, z_part, core_part):
        return (y_part * 16 + (z_part + 16) % 16) * 2 + core_part

    lats = [(j + d) % 8 for d in range(1, 8)]
    fars = []
    for y in range(2):
        for k in range(4):
            if y or k:
                fars.append(tm_of((yh + y) % 2, z + 4 * k, core))
    nears = [tm_of(yh, z + d, core) for d in (1, -1, 2, -2)]
    other = tm_of(yh, z, 1 - core)

    barrier = pltpu.get_barrier_semaphore()
    for peer in lats:
        pl.semaphore_signal(
            barrier, inc=1, device_id={"lat": peer}, device_id_type=pl.DeviceIdType.MESH
        )
    for peer in fars + nears + [other]:
        pl.semaphore_signal(
            barrier, inc=1, device_id={"tm": peer}, device_id_type=pl.DeviceIdType.MESH
        )
    pl.semaphore_wait(barrier, 7 + 7 + 4 + 1)

    def to(src, dst, send_sem, recv_sem, **peer):
        return pltpu.make_async_remote_copy(
            src_ref=src,
            dst_ref=dst,
            send_sem=send_sem,
            recv_sem=recv_sem,
            device_id=peer,
            device_id_type=pl.DeviceIdType.MESH,
        )

    copies = []
    for d, peer in enumerate(lats):
        copies.append(
            to(part_ref.at[0, :, pl.ds(0, PANEL)], got1.at[j], send.at[d], rs1.at[d], lat=peer)
        )
        copies.append(to(part_ref.at[peer], got.at[j], send.at[7 + d], rs.at[d], lat=peer))
    for copy in copies:
        copy.start()
    got[j] = part_ref[j]
    got1[j] = part_ref[0, :, :PANEL]
    for copy in copies:
        copy.wait()
    scale = F32(1.0 / math.sqrt(NLON))
    total, total1 = got[0], got1[0]
    for s in range(1, 8):
        total, total1 = total + got[s], total1 + got1[s]
    own[:, :WIDTH] = (total * scale).astype(BF16)
    own[:, WIDTH:] = (total1 * scale).astype(BF16)

    mine = (z // 4) * 2 + yh
    copies = [
        to(own, far.at[mine], send.at[d], fs.at[d], tm=peer) for d, peer in enumerate(fars)
    ]
    for copy in copies:
        copy.start()
    far[mine] = own[...]
    for copy in copies:
        copy.wait()
    pieces = [far[s].astype(F32) for s in range(8)]
    all_ref[0] = jnp.concatenate(pieces, axis=0).astype(BF16)

    top, bottom = pl.ds(0, 8), pl.ds(8, 8)
    near = [
        to(all_ref.at[0], all_ref.at[2], send.at[0], ns.at[0], tm=nears[0]),
        to(all_ref.at[0], all_ref.at[1], send.at[1], ns.at[1], tm=nears[1]),
        to(all_ref.at[0, top], all_ref.at[3, top], send.at[2], ns.at[2], tm=nears[2]),
        to(all_ref.at[0, bottom], all_ref.at[3, bottom], send.at[3], ns.at[3], tm=nears[3]),
    ]
    across = [
        to(all_ref.at[s], all_ref.at[4 + s], send2.at[s], cs.at[s], tm=other) for s in range(4)
    ]
    for copy in near:
        copy.start()
    across[0].start()
    near[0].wait_recv()
    across[2].start()
    near[1].wait_recv()
    across[1].start()
    near[2].wait_recv()
    near[3].wait_recv()
    across[3].start()
    for copy in across:
        copy.wait_recv()
    for copy in near + across:
        copy.wait_send()

    root = i // 8
    lanes = pl.ds(pl.multiple_of((i % 8) * BLOCK, BLOCK), BLOCK)

    @pl.when(j == root)
    def _():
        out = [
            to(all_ref.at[:, :, lanes], row_ref, send.at[d], ws, lat=peer)
            for d, peer in enumerate(lats)
        ]
        for copy in out:
            copy.start()
        here = pltpu.make_async_copy(all_ref.at[:, :, lanes], row_ref, keep)
        here.start()
        here.wait()
        for copy in out:
            copy.wait_send()

    @pl.when(j != root)
    def _():
        to(all_ref.at[:, :, lanes], row_ref, send.at[0], ws, lat=root).wait_recv()


def exchange(parts):
    dma = pltpu.SemaphoreType.DMA
    return pl.pallas_call(
        exchange_kernel,
        in_specs=[pl.BlockSpec(memory_space=pltpu.VMEM)],
        out_specs=[pl.BlockSpec(memory_space=pltpu.VMEM)] * 2,
        out_shape=[
            jax.ShapeDtypeStruct((8, 16, SENT), BF16),
            jax.ShapeDtypeStruct((8, 16, BLOCK), BF16),
        ],
        scratch_shapes=[
            pltpu.VMEM((8, 2, WIDTH), F32),
            pltpu.VMEM((8, 2, PANEL), F32),
            pltpu.VMEM((2, SENT), BF16),
            pltpu.VMEM((8, 2, SENT), BF16),
            dma((14,)),
            dma((7,)),
            dma((7,)),
            dma((7,)),
            dma((4,)),
            dma((4,)),
            dma(()),
            dma((4,)),
            dma(()),
        ],
        compiler_params=pltpu.CompilerParams(collective_id=0, has_side_effects=True),
        name="exchange",
    )(parts)


def split(x):
    high = x.astype(BF16)
    return high, (x - high.astype(F32)).astype(BF16)


def contract(left, right, dims):
    def dot(a, b):
        return lax.dot_general(a, b, (dims, ((), ())), preferred_element_type=F32)

    lefts = (left,) if left.dtype == BF16 else split(left)
    rights = (right,) if right.dtype == BF16 else split(right)
    total = dot(lefts[0], rights[0])
    if len(lefts) > 1:
        total = total + dot(lefts[1], rights[0])
    if len(rights) > 1:
        total = total + dot(lefts[0], rights[1])
    return total


ROWS = ((0,), (0,))
LANES = ((1,), (1,))
PLAIN = ((1,), (0,))


def eliminate(spd, rhs, upper_ref, solved_ref, panel=32, group=8):
    count, size = len(spd), BLOCK
    for b in range(count):
        upper_ref[b] = spd[b]
        solved_ref[b] = rhs[b]
    sub = lax.broadcasted_iota(jnp.int32, (panel, size), 0)
    for p in range(0, size, panel):
        x = [upper_ref[b, p : p + panel, :] for b in range(count)]
        y = [solved_ref[b, p : p + panel, :] for b in range(count)]
        scale = [jnp.ones((panel, size), F32) for _ in range(count)]
        for start in range(0, panel, group):
            column = [
                [
                    jnp.broadcast_to(x[b][:, p + start + m : p + start + m + 1], (panel, size))
                    for m in range(group)
                ]
                for b in range(count)
            ]
            for m in range(group):
                k = start + m
                for b in range(count):
                    c = column[b][m]
                    pivot = jnp.broadcast_to(c[k : k + 1, :], (panel, size))
                    factor = jnp.where(sub > k, c * (1.0 / pivot), 0.0)
                    scale[b] = jnp.where(sub == k, lax.rsqrt(pivot), scale[b])
                    for later in range(m + 1, group):
                        u = column[b][later]
                        column[b][later] = u - factor * u[k : k + 1, :]
                    x[b] = x[b] - factor * x[b][k : k + 1, :]
                    y[b] = y[b] - factor * y[b][k : k + 1, :]
        for b in range(count):
            x[b], y[b] = x[b] * scale[b], y[b] * scale[b]
            upper_ref[b, p : p + panel, :] = x[b]
            solved_ref[b, p : p + panel, :] = y[b]
            if p + panel < size:
                below = x[b][:, p + panel :]
                upper_ref[b, p + panel :, :] -= contract(below, x[b], ROWS)
                solved_ref[b, p + panel :, :] -= contract(below, y[b], ROWS)


def panel_kernel(all_ref, row_ref, win_ref, ridge_ref, out_ref, upper, solved, upper2, solved2):
    i, j = lax.axis_index("tm"), lax.axis_index("lat")
    ridge = ridge_ref[0]

    def lam_of(degree):
        return ridge * (1.0 + (degree * (degree + 1)).astype(F32) / float(LMAX * (LMAX + 1)))

    lam = lam_of(win_ref[0:1, :PANEL])
    row_id = lax.broadcasted_iota(jnp.int32, (BLOCK, BLOCK), 0)
    col_id = lax.broadcasted_iota(jnp.int32, (BLOCK, BLOCK), 1)
    eye = (row_id == col_id).astype(F32)
    inverse = F32(1.0 / NT)
    blocks = [
        all_ref[:, :, WIDTH + BLOCK * b : WIDTH + BLOCK * (b + 1)].reshape(NT, BLOCK)
        for b in range(4)
    ]
    cols = all_ref[:, :, :WIDTH].reshape(NT, WIDTH)
    rows = row_ref[...].reshape(NT, BLOCK)
    lams = [lam[:, BLOCK * b : BLOCK * (b + 1)] for b in range(4)]

    total, spd = eye, []
    for b in range(4):
        total = total + contract(blocks[b].astype(F32) * (inverse / lams[b]), blocks[b], LANES)
        spd.append(total)
    eliminate(spd, [eye] * 4, upper, solved)
    spd, rhs = [], []
    for b in range(4):
        if b == 0:
            spd.append(contract(blocks[0], blocks[0], ROWS) * inverse + eye * lams[0])
            rhs.append(blocks[0].astype(F32).T)
        else:
            low = solved[b - 1]
            first = contract(low, blocks[b], PLAIN)
            spd.append(contract(first, first, ROWS) * inverse + eye * lams[b])
            rhs.append(contract(first, low, ROWS))
    eliminate(spd, rhs, upper2, solved2)

    @pl.when(i < 4)
    def _():
        out_ref[...] = contract(solved2[i], cols, PLAIN) * inverse

    @pl.when(i >= 4)
    def _():
        low = solved[3]
        first = contract(low, rows, PLAIN)
        left = contract(first, low, ROWS)
        start = pl.multiple_of(j * WIDTH, WIDTH)
        lam_cols = lam_of(win_ref[0:1, pl.ds(start, WIDTH)])
        row_glob = i * BLOCK + lax.broadcasted_iota(jnp.int32, (BLOCK, WIDTH), 0)
        col_glob = j * WIDTH + lax.broadcasted_iota(jnp.int32, (BLOCK, WIDTH), 1)
        out_ref[...] = contract(left, cols, PLAIN) * inverse + jnp.where(
            row_glob == col_glob, lam_cols, 0.0
        )

    @pl.when(j == 0)
    def _():
        for b in range(4):
            lower = jnp.where(row_id >= col_id, upper2[b].T, 0.0)
            below = contract(rows, solved2[b], ((0,), (1,))) * inverse
            out_ref[:, BLOCK * b : BLOCK * (b + 1)] = jnp.where(
                i > b, below, jnp.where(i == b, lower, 0.0)
            )


def panel_step(everyone, rows, window, ridge):
    vmem = pl.BlockSpec(memory_space=pltpu.VMEM)
    return pl.pallas_call(
        panel_kernel,
        in_specs=[vmem, vmem, vmem, pl.BlockSpec(memory_space=pltpu.SMEM)],
        out_specs=vmem,
        out_shape=jax.ShapeDtypeStruct((BLOCK, WIDTH), F32),
        scratch_shapes=[pltpu.VMEM((4, BLOCK, BLOCK), F32)] * 4,
        name="panel",
    )(everyone, rows, window, ridge)


def on_device(fields, legendre, order_table, window_start, ridge):
    window = lax.dynamic_slice_in_dim(order_table, window_start[0], legendre.shape[1], 1)
    parts = partial_coeffs(fields, legendre, window)
    everyone, rows = exchange(parts)
    return panel_step(everyone, rows, window, ridge)


def solution(mesh):
    placed = (P("tm", "lat", None), P("lat", None), P(), P(), P())
    return jax.shard_map(
        on_device, mesh=mesh, in_specs=placed, out_specs=P("tm", "lat"), check_vma=False
    )
```

time: 478 us -> 71.6 us (0.15)
  the two profiles are of different devices: /device:TPU:16 before, /device:TPU:1 now
where the time goes in v1:
time: 71.6 us; the launch traced here: 71.2 us
  Pallas kernels  67.2 us (94%)
  local copies, waits for them, and re-layouts  2.71 us (4%)
  between operations  1.36 us (2%)
    pallas_call x1, Pallas kernels, exchange(): pl.pallas_call(exchange_kernel, in_specs=[pl.BlockSpec(memory_space=pltpu...  41.9 us
    pallas_call x1, Pallas kernels, panel_step(): pl.pallas_call(panel_kernel, in_specs=[vmem, vmem, vmem, pl.BlockSpec(mem...  14.3 us
    pallas_call x1, Pallas kernels, partial_coeffs(): pl.pallas_call(spectral_kernel, grid=(kcoef // WIDTH,), in_specs=[pl.Bloc...  11 us
    unnamed x3, local copies, waits for them, and re-layouts  1.92 us

profile of v1, /device:TPU:1, one launch (start us, length us, event | category | flops | bytes accessed | tf_op | source)
XLA Modules:
  0.0 71.2 jit_solution(1233045141191501293)
XLA Ops:
  0.0 0.0 copy-start
  1.3 0.0 copy-done
  1.4 0.8 %constant_dynamic-slice_fusion.win_ref = s32[3,8192]{1,0:T(4,128)} fusion(s32[3,16384]{1,0:T(4,128)S(1)} %copy-done, s32[]{:T(128)S(6)} %select_n.3), kind=kLoop, calls=%fused_computation | loop fusion | bytes 196612 | tf_op jit(solution)/shard_map/dynamic_slice | solution.py:378
  2.1 1.9 %copy.7.fields_ref = bf16[2,90,1440]{2,1,0:T(8,128)(2,1)} copy(bf16[2,90,1440]{2,0,1:T(2,128)(2,1)} %param.6) | data formatting | bytes 1036800 | tf_op args[0]
  4.1 11.0 %spectral.1.part_ref = f32[8,2,1024]{2,1,0:T(2,128)} custom-call(bf16[2,90,1440]{2,1,0:T(8,128)(2,1)} %copy.7.fields_ref, bf16[2,720,768]{2,1,0:T(8,128)(2,1)} %constant.6.clone.basis_ref, bf16[90,8192]{1,0:T(8,128)(2,1)} %leg_ref.1, s32[3,8192]{1,0:T(4,128)} %constant_dynamic-slice_fusion.win_ref), custom_call_target="tpu_custom_call" | custom-call | tf_op jit(solution)/shard_map/spectral/pallas_call | solution.py:74
  15.1 41.9 %exchange.1 = (bf16[8,16,1536]{2,1,0:T(8,128)(2,1)}, bf16[8,16,128]{2,1,0:T(8,128)(2,1)}) custom-call(f32[8,2,1024]{2,1,0:T(2,128)} %spectral.1.part_ref), custom_call_target="tpu_custom_call" | custom-call | tf_op jit(solution)/shard_map/exchange/pallas_call | solution.py:209
  57.0 14.3 %panel.1 = f32[128,1024]{1,0:T(8,128)} custom-call(bf16[8,16,1536]{2,1,0:T(8,128)(2,1)} %get-tuple-element.7.all_ref, bf16[8,16,128]{2,1,0:T(8,128)(2,1)} %get-tuple-element.8.row_ref, s32[3,8192]{1,0:T(4,128)} %constant_dynamic-slice_fusion.win_ref, f32[1]{0:T(128)S(6)} %copy.9.ridge_ref), custom_call_target="tpu_custom_call" | custom-call | tf_op jit(solution)/shard_map/panel/pallas_call | solution.py:367
Async XLA Ops:
  0.0 1.3 %copy-start = (s32[3,16384]{1,0:T(4,128)S(1)}, s32[3,16384]{1,0:T(4,128)}, u32[]{:S(2)}) copy-start(s32[3,16384]{1,0:T(4,128)} %param.8) | copy-start | bytes 589828

commit v2 on v1

v2 whole, which is shorter than its diff:
```python
import math

import jax
import jax.numpy as jnp
import numpy as np
from jax import lax
from jax.experimental import pallas as pl
from jax.experimental.pallas import tpu as pltpu
from jax.sharding import PartitionSpec as P

NLON = 1440
HALF = NLON // 2
LMAX = 720
NT = 128
PANEL = 512
BLOCK = 128
WIDTH = 1024
SENT = WIDTH + PANEL
LAT = 90
LATPAD = 96
DEEP = 768
CHUNK = 256
F32 = jnp.float32
BF16 = jnp.bfloat16


def half_basis():
    n = np.arange(HALF)[:, None]
    c = np.arange(HALF)[None, :]
    phase = ((n * c) % NLON).astype(np.float32) * np.float32(2.0 * math.pi / NLON)
    basis = np.zeros((2, HALF, DEEP), np.float32)
    basis[0, :, :HALF] = np.cos(phase)
    basis[1, :, :HALF] = np.sin(phase)
    return basis.astype(BF16)


FARS = (6, 0, 3, -3, -6)
NEARS = ((0, 0, 5), (1, 5, 5), (-1, 10, 5), (2, 15, 1))


def coeff_kernel(
    fields_hbm,
    basis_hbm,
    leg_hbm,
    table_hbm,
    all_ref,
    row_ref,
    fields,
    basis,
    leg,
    table,
    spectra,
    rows,
    part,
    got,
    got1,
    load,
    legs,
    lat_send,
    lat_recv,
    far_send,
    far_recv,
    near_send,
    near_recv,
    core_send,
    core_recv,
    row_send,
    row_recv,
    keep,
):
    i, j = lax.axis_index("tm"), lax.axis_index("lat")
    core, z, yh = i % 2, (i // 2) % 16, i // 32
    mesh_ids = pl.DeviceIdType.MESH

    def tm_of(y_part, z_part, core_part):
        return (y_part * 16 + (z_part + 16) % 16) * 2 + core_part

    lats = [(j + d) % 8 for d in range(1, 8)]
    other = tm_of(yh, z, 1 - core)
    greeted = [tm_of(yh, z + d, core) for d in (3, -3, 6, -6, 1, -1, 2, -2)]
    greeted += [tm_of(1 - yh, z + d, core) for d in (0, 1, -1, 2, -2)]
    greeted += [other]

    loads = [
        pltpu.make_async_copy(fields_hbm, fields, load.at[0]),
        pltpu.make_async_copy(basis_hbm.at[0], basis.at[0], load.at[1]),
        pltpu.make_async_copy(basis_hbm.at[1], basis.at[1], load.at[2]),
        pltpu.make_async_copy(table_hbm, table, load.at[3]),
    ]
    for copy in loads:
        copy.start()

    def leg_copy(k):
        cols = pl.ds(pl.multiple_of(k * WIDTH, WIDTH), WIDTH)
        return pltpu.make_async_copy(leg_hbm.at[:, cols], leg.at[k], legs.at[k])

    for k in range(8):
        leg_copy(k).start()
    barrier = pltpu.get_barrier_semaphore()
    for peer in lats:
        pl.semaphore_signal(barrier, inc=1, device_id={"lat": peer}, device_id_type=mesh_ids)
    for peer in greeted:
        pl.semaphore_signal(barrier, inc=1, device_id={"tm": peer}, device_id_type=mesh_ids)

    loads[0].wait()
    lane = lax.broadcasted_iota(jnp.int32, (1, DEEP), 1)
    sign = jnp.where(lane % 2 == 0, 1.0, -1.0).astype(F32)
    flat = fields[...].reshape(2 * LAT, NLON)
    low, high = flat[:, :HALF], flat[:, HALF:]
    for p in range(2):
        loads[1 + p].wait()
        first = jnp.dot(low, basis[p], preferred_element_type=F32)
        second = jnp.dot(high, basis[p], preferred_element_type=F32)
        both = first + sign * second
        for v in range(DEEP // 128):
            lanes = slice(v * 128, (v + 1) * 128)
            spectra[v] = both[:, lanes]
            for t in range(2):
                at = (2 * p + t) * LATPAD
                rows[at : at + LAT, lanes] = spectra[v, pl.ds(t, LAT, stride=2), :].astype(BF16)

    loads[3].wait()
    iota = lax.broadcasted_iota(jnp.int32, (CHUNK, CHUNK), 0).astype(F32).astype(BF16)
    one, zero = jnp.ones((CHUNK, CHUNK), BF16), jnp.zeros((CHUNK, CHUNK), BF16)

    def tile(k, carry):
        leg_copy(k).wait()
        window = table[:, pl.ds(pl.multiple_of(k * WIDTH, WIDTH), WIDTH)]
        for n in range(WIDTH // CHUNK):
            cols = slice(n * CHUNK, (n + 1) * CHUNK)
            order, sine_part = window[1:2, cols], window[2:3, cols]
            picked = None
            for q in range(DEEP // CHUNK):
                rel = jnp.clip(order - CHUNK * q, -1, CHUNK).astype(F32).astype(BF16)
                onehot = jnp.where(iota == rel, one, zero)
                term = jnp.dot(
                    rows[:, q * CHUNK : (q + 1) * CHUNK], onehot, preferred_element_type=F32
                )
                picked = term if picked is None else picked + term
            weights = leg[k, :, cols].astype(F32)
            for t in range(2):
                cosine = picked[t * LATPAD : t * LATPAD + LAT]
                sine = picked[(2 + t) * LATPAD : (2 + t) * LATPAD + LAT]
                chosen = jnp.where(sine_part > 0, sine, cosine)
                part[k, t : t + 1, cols] = jnp.sum(chosen * weights, axis=0, keepdims=True)
        return carry

    lax.fori_loop(0, 8, tile, 0)

    pl.semaphore_wait(barrier, 7 + 14)

    def to(src, dst, send_sem, recv_sem, **peer):
        return pltpu.make_async_remote_copy(
            src_ref=src,
            dst_ref=dst,
            send_sem=send_sem,
            recv_sem=recv_sem,
            device_id=peer,
            device_id_type=mesh_ids,
        )

    copies = []
    for d, peer in enumerate(lats):
        sems = (lat_send.at[2 * d], lat_recv.at[2 * d])
        copies.append(to(part.at[0, :, pl.ds(0, PANEL)], got1.at[j], *sems, lat=peer))
        sems = (lat_send.at[2 * d + 1], lat_recv.at[2 * d + 1])
        copies.append(to(part.at[peer], got.at[j], *sems, lat=peer))
    for copy in copies:
        copy.start()
    got[j] = part[j]
    got1[j] = part[0, :, :PANEL]
    for copy in copies:
        copy.wait_recv()
    scale = F32(1.0 / math.sqrt(NLON))
    total, total1 = got[0], got1[0]
    for s in range(1, 8):
        total, total1 = total + got[s], total1 + got1[s]
    all_ref[1, :, :WIDTH] = (total * scale).astype(BF16)
    all_ref[1, :, WIDTH:] = (total1 * scale).astype(BF16)

    far = []
    for s, a in enumerate(FARS):
        if a:
            far.append(
                to(
                    all_ref.at[1],
                    all_ref.at[s],
                    far_send.at[s],
                    far_recv.at[s],
                    tm=tm_of(yh, z - a, core),
                )
            )
    for copy in far:
        copy.start()
    for copy in far:
        copy.wait_recv()

    near, across = [], []
    for y in range(2):
        for b, at, count in NEARS:
            k = len(across)
            here = pl.ds(16 * y + at, count)
            if y or b:
                near.append(
                    to(
                        all_ref.at[pl.ds(0, count)],
                        all_ref.at[here],
                        near_send.at[k],
                        near_recv.at[k],
                        tm=tm_of(yh if y == 0 else 1 - yh, z - b, core),
                    )
                )
            else:
                near.append(None)
            across.append(
                to(
                    all_ref.at[here],
                    all_ref.at[pl.ds(32 + 16 * y + at, count)],
                    core_send.at[k],
                    core_recv.at[k],
                    tm=other,
                )
            )
    for copy in near:
        if copy is not None:
            copy.start()
    for copy, onward in zip(near, across):
        if copy is not None:
            copy.wait_recv()
        onward.start()
    for copy in across:
        copy.wait_recv()

    root = i // 8
    lanes = pl.ds(pl.multiple_of((i % 8) * BLOCK, BLOCK), BLOCK)

    @pl.when(j == root)
    def _():
        out = [
            to(all_ref.at[:, :, lanes], row_ref, row_send.at[d], row_recv, lat=peer)
            for d, peer in enumerate(lats)
        ]
        for copy in out:
            copy.start()
        here = pltpu.make_async_copy(all_ref.at[:, :, lanes], row_ref, keep)
        here.start()
        here.wait()
        for copy in out:
            copy.wait_send()

    @pl.when(j != root)
    def _():
        to(all_ref.at[:, :, lanes], row_ref, row_send.at[0], row_recv, lat=root).wait_recv()

    for copy in copies + far + [copy for copy in near if copy is not None] + across:
        copy.wait_send()


def coefficients(fields, legendre, window):
    dma = pltpu.SemaphoreType.DMA
    hbm = pl.BlockSpec(memory_space=pl.ANY)
    vmem = pl.BlockSpec(memory_space=pltpu.VMEM)
    return pl.pallas_call(
        coeff_kernel,
        in_specs=[hbm] * 4,
        out_specs=[vmem, vmem],
        out_shape=[
            jax.ShapeDtypeStruct((64, 2, SENT), BF16),
            jax.ShapeDtypeStruct((64, 2, BLOCK), BF16),
        ],
        scratch_shapes=[
            pltpu.VMEM((LAT, 2, NLON), BF16),
            pltpu.VMEM((2, HALF, DEEP), BF16),
            pltpu.VMEM((8, LAT, WIDTH), BF16),
            pltpu.VMEM((3, 8 * WIDTH), jnp.int32),
            pltpu.VMEM((DEEP // 128, 2 * LAT, 128), F32),
            pltpu.VMEM((4 * LATPAD, DEEP), BF16),
            pltpu.VMEM((8, 2, WIDTH), F32),
            pltpu.VMEM((8, 2, WIDTH), F32),
            pltpu.VMEM((8, 2, PANEL), F32),
            dma((4,)),
            dma((8,)),
            dma((14,)),
            dma((14,)),
            dma((5,)),
            dma((5,)),
            dma((8,)),
            dma((8,)),
            dma((8,)),
            dma((8,)),
            dma((7,)),
            dma(()),
            dma(()),
        ],
        compiler_params=pltpu.CompilerParams(collective_id=0, has_side_effects=True),
        name="coeffs",
    )(
        jnp.transpose(fields, (1, 0, 2)),
        jnp.asarray(half_basis()),
        legendre,
        window,
    )


def split(x):
    high = x.astype(BF16)
    return high, (x - high.astype(F32)).astype(BF16)


def contract(left, right, dims):
    def dot(a, b):
        return lax.dot_general(a, b, (dims, ((), ())), preferred_element_type=F32)

    lefts = (left,) if left.dtype == BF16 else split(left)
    rights = (right,) if right.dtype == BF16 else split(right)
    total = dot(lefts[0], rights[0])
    if len(lefts) > 1:
        total = total + dot(lefts[1], rights[0])
    if len(rights) > 1:
        total = total + dot(lefts[0], rights[1])
    return total


ROWS = ((0,), (0,))
LANES = ((1,), (1,))
PLAIN = ((1,), (0,))


def eliminate(spd, rhs, upper_ref, solved_ref, panel=32, group=8):
    count, size = len(spd), BLOCK
    for b in range(count):
        upper_ref[b] = spd[b]
        solved_ref[b] = rhs[b]
    sub = lax.broadcasted_iota(jnp.int32, (panel, size), 0)
    for p in range(0, size, panel):
        x = [upper_ref[b, p : p + panel, :] for b in range(count)]
        y = [solved_ref[b, p : p + panel, :] for b in range(count)]
        scale = [jnp.ones((panel, size), F32) for _ in range(count)]
        for start in range(0, panel, group):
            column = [
                [
                    jnp.broadcast_to(x[b][:, p + start + m : p + start + m + 1], (panel, size))
                    for m in range(group)
                ]
                for b in range(count)
            ]
            for m in range(group):
                k = start + m
                for b in range(count):
                    c = column[b][m]
                    pivot = jnp.broadcast_to(c[k : k + 1, :], (panel, size))
                    factor = jnp.where(sub > k, c * (1.0 / pivot), 0.0)
                    scale[b] = jnp.where(sub == k, lax.rsqrt(pivot), scale[b])
                    for later in range(m + 1, group):
                        u = column[b][later]
                        column[b][later] = u - factor * u[k : k + 1, :]
                    x[b] = x[b] - factor * x[b][k : k + 1, :]
                    y[b] = y[b] - factor * y[b][k : k + 1, :]
        for b in range(count):
            x[b], y[b] = x[b] * scale[b], y[b] * scale[b]
            upper_ref[b, p : p + panel, :] = x[b]
            solved_ref[b, p : p + panel, :] = y[b]
            if p + panel < size:
                below = x[b][:, p + panel :]
                upper_ref[b, p + panel :, :] -= contract(below, x[b], ROWS)
                solved_ref[b, p + panel :, :] -= contract(below, y[b], ROWS)


def panel_kernel(all_ref, row_ref, win_ref, ridge_ref, out_ref, upper, solved, upper2, solved2):
    i, j = lax.axis_index("tm"), lax.axis_index("lat")
    ridge = ridge_ref[0]

    def lam_of(degree):
        return ridge * (1.0 + (degree * (degree + 1)).astype(F32) / float(LMAX * (LMAX + 1)))

    lam = lam_of(win_ref[0:1, :PANEL])
    row_id = lax.broadcasted_iota(jnp.int32, (BLOCK, BLOCK), 0)
    col_id = lax.broadcasted_iota(jnp.int32, (BLOCK, BLOCK), 1)
    eye = (row_id == col_id).astype(F32)
    inverse = F32(1.0 / NT)
    whole = all_ref[...].reshape(NT, SENT)
    cols = whole[:, :WIDTH]
    blocks = [whole[:, WIDTH + BLOCK * b : WIDTH + BLOCK * (b + 1)] for b in range(4)]
    rows = row_ref[...].reshape(NT, BLOCK)
    lams = [lam[:, BLOCK * b : BLOCK * (b + 1)] for b in range(4)]

    total, spd = eye, []
    for b in range(4):
        total = total + contract(blocks[b].astype(F32) * (inverse / lams[b]), blocks[b], LANES)
        spd.append(total)
    eliminate(spd, [eye] * 4, upper, solved)
    spd, rhs = [], []
    for b in range(4):
        if b == 0:
            spd.append(contract(blocks[0], blocks[0], ROWS) * inverse + eye * lams[0])
            rhs.append(blocks[0].astype(F32).T)
        else:
            low = solved[b - 1]
            first = contract(low, blocks[b], PLAIN)
            spd.append(contract(first, first, ROWS) * inverse + eye * lams[b])
            rhs.append(contract(first, low, ROWS))
    eliminate(spd, rhs, upper2, solved2)

    @pl.when(i < 4)
    def _():
        out_ref[...] = contract(solved2[i], cols, PLAIN) * inverse

    @pl.when(i >= 4)
    def _():
        low = solved[3]
        first = contract(low, rows, PLAIN)
        left = contract(first, low, ROWS)
        start = pl.multiple_of(j * WIDTH, WIDTH)
        lam_cols = lam_of(win_ref[0:1, pl.ds(start, WIDTH)])
        row_glob = i * BLOCK + lax.broadcasted_iota(jnp.int32, (BLOCK, WIDTH), 0)
        col_glob = j * WIDTH + lax.broadcasted_iota(jnp.int32, (BLOCK, WIDTH), 1)
        out_ref[...] = contract(left, cols, PLAIN) * inverse + jnp.where(
            row_glob == col_glob, lam_cols, 0.0
        )

    @pl.when(j == 0)
    def _():
        for b in range(4):
            lower = jnp.where(row_id >= col_id, upper2[b].T, 0.0)
            below = contract(rows, solved2[b], ((0,), (1,))) * inverse
            out_ref[:, BLOCK * b : BLOCK * (b + 1)] = jnp.where(
                i > b, below, jnp.where(i == b, lower, 0.0)
            )


def panel_step(everyone, rows, window, ridge):
    vmem = pl.BlockSpec(memory_space=pltpu.VMEM)
    return pl.pallas_call(
        panel_kernel,
        in_specs=[vmem, vmem, vmem, pl.BlockSpec(memory_space=pltpu.SMEM)],
        out_specs=vmem,
        out_shape=jax.ShapeDtypeStruct((BLOCK, WIDTH), F32),
        scratch_shapes=[pltpu.VMEM((4, BLOCK, BLOCK), F32)] * 4,
        name="panel",
    )(everyone, rows, window, ridge)


def on_device(fields, legendre, order_table, window_start, ridge):
    window = lax.dynamic_slice_in_dim(order_table, window_start[0], legendre.shape[1], 1)
    everyone, rows = coefficients(fields, legendre, window)
    return panel_step(everyone, rows, window, ridge)


def solution(mesh):
    placed = (P("tm", "lat", None), P("lat", None), P(), P(), P())
    return jax.shard_map(
        on_device, mesh=mesh, in_specs=placed, out_specs=P("tm", "lat"), check_vma=False
    )
```

time: 71.6 us -> 60.4 us (0.84)
  Pallas kernels: 67.2 us -> 58.1 us
  local copies, waits for them, and re-layouts: 2.71 us -> 0.79 us
    pallas_call x2 -> x1, Pallas kernels: 52.9 us -> 43.8 us  [coefficients(): pl.pallas_call(coeff_kernel, in_specs=[hbm] * 4, out_specs=[vmem, vmem],...]
    unnamed x3 -> x2, local copies, waits for them, and re-layouts: 1.92 us -> 0.01 us
where the time goes in v2:
time: 60.4 us; the launch traced here: 60.3 us
  Pallas kernels  58.1 us (96%)
  between operations  1.36 us (2%)
  local copies, waits for them, and re-layouts  0.79 us (1%)
    pallas_call x1, Pallas kernels, coefficients(): pl.pallas_call(coeff_kernel, in_specs=[hbm] * 4, out_specs=[vmem, vmem],...  43.8 us
    pallas_call x1, Pallas kernels, panel_step(): pl.pallas_call(panel_kernel, in_specs=[vmem, vmem, vmem, pl.BlockSpec(mem...  14.4 us

profile of v2, /device:TPU:1, one launch (start us, length us, event | category | flops | bytes accessed | tf_op | source)
XLA Modules:
  0.0 60.3 jit_solution(3647527298360922157)
XLA Ops:
  0.0 0.0 copy-start
  1.3 0.0 copy-done
  1.4 0.8 %constant_dynamic-slice_fusion.table_hbm.win_ref = s32[3,8192]{1,0:T(4,128)} fusion(s32[3,16384]{1,0:T(4,128)S(1)} %copy-done, s32[]{:T(128)S(6)} %select_n.3), kind=kLoop, calls=%fused_computation | loop fusion | bytes 196612 | tf_op jit(solution)/shard_map/dynamic_slice | solution.py:444
  2.1 43.8 %coeffs.1 = (bf16[64,2,1536]{2,1,0:T(2,128)(2,1)}, bf16[64,2,128]{2,1,0:T(2,128)(2,1)}) custom-call(bf16[90,2,1440]{2,1,0:T(2,128)(2,1)} %bitcast.5, bf16[2,720,768]{2,1,0:T(8,128)(2,1)} %constant.6.clone.basis_hbm, bf16[90,8192]{1,0:T(8,128)(2,1)} %leg_hbm.1, s32[3,8192]{1,0:T(4,128)} %constant_dynamic-slice_fusion.table_hbm.win_ref), custom_call_target="tpu_custom_call" | custom-call | tf_op jit(solution)/shard_map/coeffs/pallas_call | solution.py:263
  45.9 14.4 %panel.1 = f32[128,1024]{1,0:T(8,128)} custom-call(bf16[64,2,1536]{2,1,0:T(2,128)(2,1)} %get-tuple-element.7.all_ref, bf16[64,2,128]{2,1,0:T(2,128)(2,1)} %get-tuple-element.8.row_ref, s32[3,8192]{1,0:T(4,128)} %constant_dynamic-slice_fusion.table_hbm.win_ref, f32[1]{0:T(128)S(6)} %copy.8.ridge_ref), custom_call_target="tpu_custom_call" | custom-call | tf_op jit(solution)/shard_map/panel/pallas_call | solution.py:433
Async XLA Ops:
  0.0 1.3 %copy-start = (s32[3,16384]{1,0:T(4,128)S(1)}, s32[3,16384]{1,0:T(4,128)}, u32[]{:S(2)}) copy-start(s32[3,16384]{1,0:T(4,128)} %param.8) | copy-start | bytes 589828

commit v3 on v2

v3 whole, which is shorter than its diff:
```python
import math

import jax
import jax.numpy as jnp
import numpy as np
from jax import lax
from jax.experimental import pallas as pl
from jax.experimental.pallas import tpu as pltpu
from jax.sharding import PartitionSpec as P

NLON = 1440
HALF = NLON // 2
LMAX = 720
NT = 128
PANEL = 512
BLOCK = 128
WIDTH = 1024
LAT = 90
LATPAD = 96
DEEP = 768
CHUNK = 256
F32 = jnp.float32
BF16 = jnp.bfloat16


def half_basis():
    n = np.arange(HALF)[:, None]
    c = np.arange(HALF)[None, :]
    phase = ((n * c) % NLON).astype(np.float32) * np.float32(2.0 * math.pi / NLON)
    basis = np.zeros((2, HALF, DEEP), np.float32)
    basis[0, :, :HALF] = np.cos(phase)
    basis[1, :, :HALF] = np.sin(phase)
    return basis.astype(BF16)


def split(x):
    high = x.astype(BF16)
    return high, (x - high.astype(F32)).astype(BF16)


def contract(left, right, dims):
    def dot(a, b):
        return lax.dot_general(a, b, (dims, ((), ())), preferred_element_type=F32)

    lefts = (left,) if left.dtype == BF16 else split(left)
    rights = (right,) if right.dtype == BF16 else split(right)
    total = dot(lefts[0], rights[0])
    if len(lefts) > 1:
        total = total + dot(lefts[1], rights[0])
    if len(rights) > 1:
        total = total + dot(lefts[0], rights[1])
    return total


ROWS = ((0,), (0,))
LANES = ((1,), (1,))
PLAIN = ((1,), (0,))


def eliminate(spd, rhs, upper_ref, solved_ref, between=(), panel=32):
    count, size = len(spd), BLOCK
    for b in range(count):
        upper_ref[b] = spd[b]
        solved_ref[b] = rhs[b]
    sub = lax.broadcasted_iota(jnp.int32, (8, size), 0)
    pieces = panel // 8
    for p in range(0, size, panel):
        at = [slice(p + 8 * r, p + 8 * r + 8) for r in range(pieces)]
        x = [[upper_ref[b, rows, :] for rows in at] for b in range(count)]
        y = [[solved_ref[b, rows, :] for rows in at] for b in range(count)]
        for g in range(pieces):
            lane = p + 8 * g
            column = [
                [
                    [
                        jnp.broadcast_to(x[b][r][:, lane + m : lane + m + 1], (8, size))
                        for r in range(g, pieces)
                    ]
                    for m in range(8)
                ]
                for b in range(count)
            ]
            scale = [jnp.ones((8, size), F32) for _ in range(count)]
            for m in range(8):
                for b in range(count):
                    c = column[b][m]
                    root = lax.rsqrt(jnp.broadcast_to(c[0][m : m + 1, :], (8, size)))
                    inverse = root * root
                    scale[b] = jnp.where(sub == m, root, scale[b])
                    x_row = jnp.broadcast_to(x[b][g][m : m + 1, :], (8, size))
                    y_row = jnp.broadcast_to(y[b][g][m : m + 1, :], (8, size))
                    u_rows = [
                        jnp.broadcast_to(column[b][later][0][m : m + 1, :], (8, size))
                        for later in range(m + 1, 8)
                    ]
                    for r in range(g, pieces):
                        factor = c[r - g] * inverse
                        if r == g:
                            factor = jnp.where(sub > m, factor, 0.0)
                        for later in range(m + 1, 8):
                            u = column[b][later]
                            u[r - g] = u[r - g] - factor * u_rows[later - m - 1]
                        x[b][r] = x[b][r] - factor * x_row
                        y[b][r] = y[b][r] - factor * y_row
            for b in range(count):
                x[b][g], y[b][g] = x[b][g] * scale[b], y[b][g] * scale[b]
                upper_ref[b, at[g], :] = x[b][g]
                solved_ref[b, at[g], :] = y[b][g]
        if p + panel < size:
            for b in range(count):
                xs, ys = jnp.concatenate(x[b], axis=0), jnp.concatenate(y[b], axis=0)
                below = xs[:, p + panel :]
                upper_ref[b, p + panel :, :] -= contract(below, xs, ROWS)
                solved_ref[b, p + panel :, :] -= contract(below, ys, ROWS)
        if p // panel < len(between):
            between[p // panel]()


FARS = (6, 0, 3, -3, -6)
NEARS = ((0, 0, 5), (1, 5, 5), (-1, 10, 5), (2, 15, 1))


def whole_kernel(
    fields_hbm,
    basis_hbm,
    leg_hbm,
    table_hbm,
    ridge_ref,
    out_ref,
    firsts,
    wides,
    row_ref,
    fields,
    basis,
    leg,
    table,
    spectra,
    rows,
    part,
    got,
    got1,
    load,
    legs,
    lat_send,
    lat_recv,
    far_send,
    far_recv,
    near_send,
    near_recv,
    core_send,
    core_recv,
    row_send,
    row_recv,
    keep,
    upper,
    solved,
    upper2,
    solved2,
):
    i, j = lax.axis_index("tm"), lax.axis_index("lat")
    core, z, yh = i % 2, (i // 2) % 16, i // 32
    mesh_ids = pl.DeviceIdType.MESH

    def tm_of(y_part, z_part, core_part):
        return (y_part * 16 + (z_part + 16) % 16) * 2 + core_part

    lats = [(j + d) % 8 for d in range(1, 8)]
    other = tm_of(yh, z, 1 - core)
    greeted = [tm_of(yh, z + d, core) for d in (3, -3, 6, -6, 1, -1, 2, -2)]
    greeted += [tm_of(1 - yh, z + d, core) for d in (0, 1, -1, 2, -2)]
    greeted += [other]

    loads = [
        pltpu.make_async_copy(fields_hbm, fields, load.at[0]),
        pltpu.make_async_copy(basis_hbm.at[0], basis.at[0], load.at[1]),
        pltpu.make_async_copy(basis_hbm.at[1], basis.at[1], load.at[2]),
        pltpu.make_async_copy(table_hbm, table, load.at[3]),
    ]
    for copy in loads:
        copy.start()

    def leg_copy(k):
        cols = pl.ds(pl.multiple_of(k * WIDTH, WIDTH), WIDTH)
        return pltpu.make_async_copy(leg_hbm.at[:, cols], leg.at[k], legs.at[k])

    for k in range(8):
        leg_copy(k).start()
    barrier = pltpu.get_barrier_semaphore()
    for peer in lats:
        pl.semaphore_signal(barrier, inc=1, device_id={"lat": peer}, device_id_type=mesh_ids)
    for peer in greeted:
        pl.semaphore_signal(barrier, inc=1, device_id={"tm": peer}, device_id_type=mesh_ids)

    loads[0].wait()
    lane = lax.broadcasted_iota(jnp.int32, (1, DEEP), 1)
    sign = jnp.where(lane % 2 == 0, 1.0, -1.0).astype(F32)
    flat = fields[...].reshape(2 * LAT, NLON)
    low, high = flat[:, :HALF], flat[:, HALF:]
    for p in range(2):
        loads[1 + p].wait()
        first = jnp.dot(low, basis[p], preferred_element_type=F32)
        second = jnp.dot(high, basis[p], preferred_element_type=F32)
        both = first + sign * second
        for v in range(DEEP // 128):
            lanes = slice(v * 128, (v + 1) * 128)
            spectra[v] = both[:, lanes]
            for t in range(2):
                at = (2 * p + t) * LATPAD
                rows[at : at + LAT, lanes] = spectra[v, pl.ds(t, LAT, stride=2), :].astype(BF16)

    loads[3].wait()
    iota = lax.broadcasted_iota(jnp.int32, (CHUNK, CHUNK), 0).astype(F32).astype(BF16)
    one, zero = jnp.ones((CHUNK, CHUNK), BF16), jnp.zeros((CHUNK, CHUNK), BF16)

    def tile(k, carry):
        leg_copy(k).wait()
        window = table[:, pl.ds(pl.multiple_of(k * WIDTH, WIDTH), WIDTH)]
        for n in range(WIDTH // CHUNK):
            cols = slice(n * CHUNK, (n + 1) * CHUNK)
            order, sine_part = window[1:2, cols], window[2:3, cols]
            picked = None
            for q in range(DEEP // CHUNK):
                rel = jnp.clip(order - CHUNK * q, -1, CHUNK).astype(F32).astype(BF16)
                onehot = jnp.where(iota == rel, one, zero)
                term = jnp.dot(
                    rows[:, q * CHUNK : (q + 1) * CHUNK], onehot, preferred_element_type=F32
                )
                picked = term if picked is None else picked + term
            weights = leg[k, :, cols].astype(F32)
            for t in range(2):
                cosine = picked[t * LATPAD : t * LATPAD + LAT]
                sine = picked[(2 + t) * LATPAD : (2 + t) * LATPAD + LAT]
                chosen = jnp.where(sine_part > 0, sine, cosine)
                part[k, t : t + 1, cols] = jnp.sum(chosen * weights, axis=0, keepdims=True)
        return carry

    lax.fori_loop(0, 8, tile, 0)

    pl.semaphore_wait(barrier, 7 + 14)

    def to(src, dst, send_sem, recv_sem, **peer):
        return pltpu.make_async_remote_copy(
            src_ref=src,
            dst_ref=dst,
            send_sem=send_sem,
            recv_sem=recv_sem,
            device_id=peer,
            device_id_type=mesh_ids,
        )

    sets = (firsts, wides)
    parts = ((got1, PANEL), (got, WIDTH))
    lat_copies = ([], [])
    for n, (landing, width) in enumerate(parts):
        for d, peer in enumerate(lats):
            src = part.at[0, :, pl.ds(0, PANEL)] if n == 0 else part.at[peer]
            k = 7 * n + d
            lat_copies[n].append(
                to(src, landing.at[j], lat_send.at[k], lat_recv.at[k], lat=peer)
            )
        for copy in lat_copies[n]:
            copy.start()
    got1[j] = part[0, :, :PANEL]
    got[j] = part[j]

    scale = F32(1.0 / math.sqrt(NLON))
    far = ([], [])
    for n, (landing, _) in enumerate(parts):
        for copy in lat_copies[n]:
            copy.wait_recv()
        total = landing[0]
        for s in range(1, 8):
            total = total + landing[s]
        sets[n][1] = (total * scale).astype(BF16)
        for s, a in enumerate(FARS):
            if a:
                far[n].append(
                    to(
                        sets[n].at[1],
                        sets[n].at[s],
                        far_send.at[5 * n + s],
                        far_recv.at[5 * n + s],
                        tm=tm_of(yh, z - a, core),
                    )
                )
        for copy in far[n]:
            copy.start()

    near, across = ([], []), ([], [])
    for n in range(2):
        for y in range(2):
            for b, at, count in NEARS:
                k = 8 * n + len(across[n])
                here = pl.ds(16 * y + at, count)
                if y or b:
                    near[n].append(
                        to(
                            sets[n].at[pl.ds(0, count)],
                            sets[n].at[here],
                            near_send.at[k],
                            near_recv.at[k],
                            tm=tm_of(yh if y == 0 else 1 - yh, z - b, core),
                        )
                    )
                else:
                    near[n].append(None)
                across[n].append(
                    to(
                        sets[n].at[here],
                        sets[n].at[pl.ds(32 + 16 * y + at, count)],
                        core_send.at[k],
                        core_recv.at[k],
                        tm=other,
                    )
                )
        for copy in far[n]:
            copy.wait_recv()
        for copy in near[n]:
            if copy is not None:
                copy.start()
        across[n][0].start()

    def pass_on(n):
        for copy, onward in zip(near[n][1:], across[n][1:]):
            copy.wait_recv()
            onward.start()

    pass_on(0)
    for copy in across[0]:
        copy.wait_recv()

    root = i // 8
    lanes = pl.ds(pl.multiple_of((i % 8) * BLOCK, BLOCK), BLOCK)
    row_copies = [
        to(wides.at[:, :, lanes], row_ref, row_send.at[d], row_recv, lat=peer)
        for d, peer in enumerate(lats)
    ]
    here = pltpu.make_async_copy(wides.at[:, :, lanes], row_ref, keep)

    def send_rows():
        for copy in across[1]:
            copy.wait_recv()

        @pl.when(j == root)
        def _():
            for copy in row_copies:
                copy.start()
            here.start()

    def wait_rows():
        @pl.when(j == root)
        def _():
            here.wait()
            for copy in row_copies:
                copy.wait_send()

        @pl.when(j != root)
        def _():
            to(wides.at[:, :, lanes], row_ref, row_send.at[0], row_recv, lat=root).wait_recv()

    ridge = ridge_ref[0]

    def lam_of(degree):
        return ridge * (1.0 + (degree * (degree + 1)).astype(F32) / float(LMAX * (LMAX + 1)))

    lam = lam_of(table[0:1, :PANEL])
    row_id = lax.broadcasted_iota(jnp.int32, (BLOCK, BLOCK), 0)
    col_id = lax.broadcasted_iota(jnp.int32, (BLOCK, BLOCK), 1)
    eye = (row_id == col_id).astype(F32)
    inverse = F32(1.0 / NT)
    first_cols = firsts[...].reshape(NT, PANEL)
    blocks = [first_cols[:, BLOCK * b : BLOCK * (b + 1)] for b in range(4)]
    lams = [lam[:, BLOCK * b : BLOCK * (b + 1)] for b in range(4)]

    total, spd = eye, []
    for b in range(4):
        total = total + contract(blocks[b].astype(F32) * (inverse / lams[b]), blocks[b], LANES)
        spd.append(total)
    eliminate(spd, [eye] * 4, upper, solved, (lambda: pass_on(1), lambda: None, send_rows))
    spd, rhs = [], []
    for b in range(4):
        if b == 0:
            spd.append(contract(blocks[0], blocks[0], ROWS) * inverse + eye * lams[0])
            rhs.append(blocks[0].astype(F32).T)
        else:
            low = solved[b - 1]
            first = contract(low, blocks[b], PLAIN)
            spd.append(contract(first, first, ROWS) * inverse + eye * lams[b])
            rhs.append(contract(first, low, ROWS))
    eliminate(spd, rhs, upper2, solved2)
    wait_rows()
    cols = wides[...].reshape(NT, WIDTH)
    rows_own = row_ref[...].reshape(NT, BLOCK)

    @pl.when(i < 4)
    def _():
        out_ref[...] = contract(solved2[jnp.minimum(i, 3)], cols, PLAIN) * inverse

    @pl.when(i >= 4)
    def _():
        low = solved[3]
        first = contract(low, rows_own, PLAIN)
        left = contract(first, low, ROWS)
        own_cols = pl.ds(pl.multiple_of(j * WIDTH, WIDTH), WIDTH)
        lam_cols = lam_of(table[0:1, own_cols])
        row_glob = i * BLOCK + lax.broadcasted_iota(jnp.int32, (BLOCK, WIDTH), 0)
        col_glob = j * WIDTH + lax.broadcasted_iota(jnp.int32, (BLOCK, WIDTH), 1)
        out_ref[...] = contract(left, cols, PLAIN) * inverse + jnp.where(
            row_glob == col_glob, lam_cols, 0.0
        )

    @pl.when(j == 0)
    def _():
        for b in range(4):
            lower = jnp.where(row_id >= col_id, upper2[b].T, 0.0)
            below = contract(rows_own, solved2[b], ((0,), (1,))) * inverse
            out_ref[:, BLOCK * b : BLOCK * (b + 1)] = jnp.where(
                i > b, below, jnp.where(i == b, lower, 0.0)
            )

    sent = lat_copies[0] + lat_copies[1] + far[0] + far[1] + across[0] + across[1]
    for copy in sent + near[0][1:] + near[1][1:]:
        copy.wait_send()


def factored_tile(fields, legendre, window, ridge):
    dma = pltpu.SemaphoreType.DMA
    hbm = pl.BlockSpec(memory_space=pl.ANY)
    vmem = pl.BlockSpec(memory_space=pltpu.VMEM)
    return pl.pallas_call(
        whole_kernel,
        in_specs=[hbm] * 4 + [pl.BlockSpec(memory_space=pltpu.SMEM)],
        out_specs=vmem,
        out_shape=jax.ShapeDtypeStruct((BLOCK, WIDTH), F32),
        scratch_shapes=[
            pltpu.VMEM((64, 2, PANEL), BF16),
            pltpu.VMEM((64, 2, WIDTH), BF16),
            pltpu.VMEM((64, 2, BLOCK), BF16),
            pltpu.VMEM((LAT, 2, NLON), BF16),
            pltpu.VMEM((2, HALF, DEEP), BF16),
            pltpu.VMEM((8, LAT, WIDTH), BF16),
            pltpu.VMEM((3, 8 * WIDTH), jnp.int32),
            pltpu.VMEM((DEEP // 128, 2 * LAT, 128), F32),
            pltpu.VMEM((4 * LATPAD, DEEP), BF16),
            pltpu.VMEM((8, 2, WIDTH), F32),
            pltpu.VMEM((8, 2, WIDTH), F32),
            pltpu.VMEM((8, 2, PANEL), F32),
            dma((4,)),
            dma((8,)),
            dma((14,)),
            dma((14,)),
            dma((10,)),
            dma((10,)),
            dma((16,)),
            dma((16,)),
            dma((16,)),
            dma((16,)),
            dma((7,)),
            dma(()),
            dma(()),
        ]
        + [pltpu.VMEM((4, BLOCK, BLOCK), F32)] * 4,
        compiler_params=pltpu.CompilerParams(collective_id=0, has_side_effects=True),
        name="factored",
    )(
        jnp.transpose(fields, (1, 0, 2)),
        jnp.asarray(half_basis()),
        legendre,
        window,
        ridge,
    )


def on_device(fields, legendre, order_table, window_start, ridge):
    window = lax.dynamic_slice_in_dim(order_table, window_start[0], legendre.shape[1], 1)
    return factored_tile(fields, legendre, window, ridge)


def solution(mesh):
    placed = (P("tm", "lat", None), P("lat", None), P(), P(), P())
    return jax.shard_map(
        on_device, mesh=mesh, in_specs=placed, out_specs=P("tm", "lat"), check_vma=False
    )
```

time: 60.4 us -> 58.2 us (0.964)
  Pallas kernels: 58.1 us -> 54 us
  local copies, waits for them, and re-layouts: 0.79 us -> 2.69 us
    pallas_call x2 -> x1, Pallas kernels: 58.1 us -> 54 us  [factored_tile(): pl.pallas_call(whole_kernel, in_specs=[hbm] * 4 + [pl.BlockSpec(memory_sp...]
    unnamed x2 -> x3, local copies, waits for them, and re-layouts: 0.01 us -> 1.89 us
where the time goes in v3:
time: 58.2 us; the launch traced here: 58 us
  Pallas kernels  54 us (93%)
  local copies, waits for them, and re-layouts  2.69 us (5%)
  between operations  1.36 us (2%)
    pallas_call x1, Pallas kernels, factored_tile(): pl.pallas_call(whole_kernel, in_specs=[hbm] * 4 + [pl.BlockSpec(memory_sp...  54 us
    unnamed x3, local copies, waits for them, and re-layouts  1.89 us

profile of v3, /device:TPU:1, one launch (start us, length us, event | category | flops | bytes accessed | tf_op | source)
XLA Modules:
  0.0 58.0 jit_solution(12119828592309636962)
XLA Ops:
  0.0 0.0 copy-start
  1.3 0.0 copy-done
  1.4 0.8 %constant_dynamic-slice_fusion.table_hbm = s32[3,8192]{1,0:T(4,128)} fusion(s32[3,16384]{1,0:T(4,128)S(1)} %copy-done, s32[]{:T(128)S(6)} %select_n.3), kind=kLoop, calls=%fused_computation | loop fusion | bytes 196612 | tf_op jit(solution)/shard_map/dynamic_slice | solution.py:475
  2.2 54.0 %factored.1 = f32[128,1024]{1,0:T(8,128)} custom-call(bf16[90,2,1440]{2,1,0:T(2,128)(2,1)} %bitcast.5, bf16[2,720,768]{2,1,0:T(8,128)(2,1)} %constant.6.clone.basis_hbm, bf16[90,8192]{1,0:T(8,128)(2,1)} %leg_hbm.1, s32[3,8192]{1,0:T(4,128)} %constant_dynamic-slice_fusion.table_hbm, f32[1]{0:T(128)S(6)} %copy.9.ridge_ref), custom_call_target="tpu_custom_call" | custom-call | tf_op jit(solution)/shard_map/factored/pallas_call | solution.py:430
  56.1 1.9 %copy.10 = f32[128,1024]{1,0:T(8,128)} copy(f32[128,1024]{1,0:T(8,128)} %factored.1) | data formatting | bytes 1048576
Async XLA Ops:
  0.0 1.3 %copy-start = (s32[3,16384]{1,0:T(4,128)S(1)}, s32[3,16384]{1,0:T(4,128)}, u32[]{:S(2)}) copy-start(s32[3,16384]{1,0:T(4,128)} %param.8) | copy-start | bytes 589828

commit v4 on v3

--- a/solution.py
+++ b/solution.py
@@ -212,29 +212,35 @@
     iota = lax.broadcasted_iota(jnp.int32, (CHUNK, CHUNK), 0).astype(F32).astype(BF16)
     one, zero = jnp.ones((CHUNK, CHUNK), BF16), jnp.zeros((CHUNK, CHUNK), BF16)
 
+    def pick(k, window, n):
+        cols = slice(n * CHUNK, (n + 1) * CHUNK)
+        order, sine_part = window[1:2, cols], window[2:3, cols]
+        picked = None
+        for q in range(DEEP // CHUNK):
+            rel = jnp.clip(order - CHUNK * q, -1, CHUNK).astype(F32).astype(BF16)
+            onehot = jnp.where(iota == rel, one, zero)
+            term = jnp.dot(
+                rows[:, q * CHUNK : (q + 1) * CHUNK], onehot, preferred_element_type=F32
+            )
+            picked = term if picked is None else picked + term
+        weights = leg[k, :, cols].astype(F32)
+        for t in range(2):
+            cosine = picked[t * LATPAD : t * LATPAD + LAT]
+            sine = picked[(2 + t) * LATPAD : (2 + t) * LATPAD + LAT]
+            chosen = jnp.where(sine_part > 0, sine, cosine)
+            part[k, t : t + 1, cols] = jnp.sum(chosen * weights, axis=0, keepdims=True)
+
     def tile(k, carry):
         leg_copy(k).wait()
         window = table[:, pl.ds(pl.multiple_of(k * WIDTH, WIDTH), WIDTH)]
         for n in range(WIDTH // CHUNK):
-            cols = slice(n * CHUNK, (n + 1) * CHUNK)
-            order, sine_part = window[1:2, cols], window[2:3, cols]
-            picked = None
-            for q in range(DEEP // CHUNK):
-                rel = jnp.clip(order - CHUNK * q, -1, CHUNK).astype(F32).astype(BF16)
-                onehot = jnp.where(iota == rel, one, zero)
-                term = jnp.dot(
-                    rows[:, q * CHUNK : (q + 1) * CHUNK], onehot, preferred_element_type=F32
-                )
-                picked = term if picked is None else picked + term
-            weights = leg[k, :, cols].astype(F32)
-            for t in range(2):
-                cosine = picked[t * LATPAD : t * LATPAD + LAT]
-                sine = picked[(2 + t) * LATPAD : (2 + t) * LATPAD + LAT]
-                chosen = jnp.where(sine_part > 0, sine, cosine)
-                part[k, t : t + 1, cols] = jnp.sum(chosen * weights, axis=0, keepdims=True)
+            pick(k, window, n)
         return carry
 
-    lax.fori_loop(0, 8, tile, 0)
+    leg_copy(0).wait()
+    window = table[:, :WIDTH]
+    for n in range(PANEL // CHUNK):
+        pick(0, window, n)
 
     pl.semaphore_wait(barrier, 7 + 14)
 
@@ -249,28 +255,27 @@
         )
 
     sets = (firsts, wides)
-    parts = ((got1, PANEL), (got, WIDTH))
-    lat_copies = ([], [])
-    for n, (landing, width) in enumerate(parts):
+    parts = (got1, got)
+    lat_copies, far = ([], []), ([], [])
+    scale = F32(1.0 / math.sqrt(NLON))
+
+    def send_parts(n):
         for d, peer in enumerate(lats):
             src = part.at[0, :, pl.ds(0, PANEL)] if n == 0 else part.at[peer]
             k = 7 * n + d
             lat_copies[n].append(
-                to(src, landing.at[j], lat_send.at[k], lat_recv.at[k], lat=peer)
+                to(src, parts[n].at[j], lat_send.at[k], lat_recv.at[k], lat=peer)
             )
         for copy in lat_copies[n]:
             copy.start()
-    got1[j] = part[0, :, :PANEL]
-    got[j] = part[j]
-
-    scale = F32(1.0 / math.sqrt(NLON))
-    far = ([], [])
-    for n, (landing, _) in enumerate(parts):
+        parts[n][j] = part[0, :, :PANEL] if n == 0 else part[j]
+
+    def send_far(n):
         for copy in lat_copies[n]:
             copy.wait_recv()
-        total = landing[0]
+        total = parts[n][0]
         for s in range(1, 8):
-            total = total + landing[s]
+            total = total + parts[n][s]
         sets[n][1] = (total * scale).astype(BF16)
         for s, a in enumerate(FARS):
             if a:
@@ -285,6 +290,14 @@
                 )
         for copy in far[n]:
             copy.start()
+
+    send_parts(0)
+    for n in range(PANEL // CHUNK, WIDTH // CHUNK):
+        pick(0, window, n)
+    lax.fori_loop(1, 4, tile, 0)
+    send_far(0)
+    lax.fori_loop(4, 8, tile, 0)
+    send_parts(1)
 
     near, across = ([], []), ([], [])
     for n in range(2):
@@ -313,6 +326,8 @@
                         tm=other,
                     )
                 )
+
+    def send_near(n):
         for copy in far[n]:
             copy.wait_recv()
         for copy in near[n]:
@@ -325,6 +340,8 @@
             copy.wait_recv()
             onward.start()
 
+    send_near(0)
+    send_far(1)
     pass_on(0)
     for copy in across[0]:
         copy.wait_recv()
@@ -376,7 +393,8 @@
     for b in range(4):
         total = total + contract(blocks[b].astype(F32) * (inverse / lams[b]), blocks[b], LANES)
         spd.append(total)
-    eliminate(spd, [eye] * 4, upper, solved, (lambda: pass_on(1), lambda: None, send_rows))
+    eliminate(spd, [eye] * 4, upper, solved, (lambda: send_near(1),))
+    pass_on(1)
     spd, rhs = [], []
     for b in range(4):
         if b == 0:
@@ -387,7 +405,7 @@
             first = contract(low, blocks[b], PLAIN)
             spd.append(contract(first, first, ROWS) * inverse + eye * lams[b])
             rhs.append(contract(first, low, ROWS))
-    eliminate(spd, rhs, upper2, solved2)
+    eliminate(spd, rhs, upper2, solved2, (send_rows,))
     wait_rows()
     cols = wides[...].reshape(NT, WIDTH)
     rows_own = row_ref[...].reshape(NT, BLOCK)
@@ -431,7 +449,7 @@
         whole_kernel,
         in_specs=[hbm] * 4 + [pl.BlockSpec(memory_space=pltpu.SMEM)],
         out_specs=vmem,
-        out_shape=jax.ShapeDtypeStruct((BLOCK, WIDTH), F32),
+        out_shape=pltpu.VMEM((BLOCK, WIDTH), F32),
         scratch_shapes=[
             pltpu.VMEM((64, 2, PANEL), BF16),
             pltpu.VMEM((64, 2, WIDTH), BF16),

time: 58.2 us -> 51.4 us (0.88)
  Pallas kernels: 54 us -> 48.3 us
  local copies, waits for them, and re-layouts: 2.69 us -> 1.6 us
    pallas_call x1, Pallas kernels: 54 us -> 48.3 us  [factored_tile(): pl.pallas_call(whole_kernel, in_specs=[hbm] * 4 + [pl.BlockSpec(memory_sp...]
    unnamed x3, local copies, waits for them, and re-layouts: 1.89 us -> 0.8 us
where the time goes in v4:
time: 51.4 us; the launch traced here: 51.3 us
  Pallas kernels  48.3 us (94%)
  local copies, waits for them, and re-layouts  1.6 us (3%)
  between operations  1.36 us (3%)
    pallas_call x1, Pallas kernels, factored_tile(): pl.pallas_call(whole_kernel, in_specs=[hbm] * 4 + [pl.BlockSpec(memory_sp...  48.3 us

profile of v4, /device:TPU:1, one launch (start us, length us, event | category | flops | bytes accessed | tf_op | source)
XLA Modules:
  0.0 51.3 jit_solution(15888531636911239233)
XLA Ops:
  0.0 0.0 copy-start
  1.3 0.0 copy-done
  1.4 0.8 %constant_dynamic-slice_fusion.table_hbm = s32[3,8192]{1,0:T(4,128)} fusion(s32[3,16384]{1,0:T(4,128)S(1)} %copy-done, s32[]{:T(128)S(6)} %select_n.3), kind=kLoop, calls=%fused_computation | loop fusion | bytes 196612 | tf_op jit(solution)/shard_map/dynamic_slice | solution.py:493
  2.2 48.3 %factored.1 = f32[128,1024]{1,0:T(8,128)S(1)} custom-call(bf16[90,2,1440]{2,1,0:T(2,128)(2,1)} %bitcast.5, bf16[2,720,768]{2,1,0:T(8,128)(2,1)} %constant.6.clone.basis_hbm, bf16[90,8192]{1,0:T(8,128)(2,1)} %leg_hbm.1, s32[3,8192]{1,0:T(4,128)} %constant_dynamic-slice_fusion.table_hbm, f32[1]{0:T(128)S(6)} %copy.10.ridge_ref), custom_call_target="tpu_custom_call" | custom-call | tf_op jit(solution)/shard_map/factored/pallas_call | solution.py:448
  50.5 0.8 %copy.8 = f32[128,1024]{1,0:T(8,128)} copy(f32[128,1024]{1,0:T(8,128)S(1)} %factored.1) | data formatting | bytes 1048576
Async XLA Ops:
  0.0 1.3 %copy-start = (s32[3,16384]{1,0:T(4,128)S(1)}, s32[3,16384]{1,0:T(4,128)}, u32[]{:S(2)}) copy-start(s32[3,16384]{1,0:T(4,128)} %param.8) | copy-start | bytes 589828

commit v5 on v4

--- a/solution.py
+++ b/solution.py
@@ -294,9 +294,9 @@
     send_parts(0)
     for n in range(PANEL // CHUNK, WIDTH // CHUNK):
         pick(0, window, n)
-    lax.fori_loop(1, 4, tile, 0)
+    lax.fori_loop(1, 6, tile, 0)
     send_far(0)
-    lax.fori_loop(4, 8, tile, 0)
+    lax.fori_loop(6, 8, tile, 0)
     send_parts(1)
 
     near, across = ([], []), ([], [])
@@ -345,6 +345,7 @@
     pass_on(0)
     for copy in across[0]:
         copy.wait_recv()
+    send_near(1)
 
     root = i // 8
     lanes = pl.ds(pl.multiple_of((i % 8) * BLOCK, BLOCK), BLOCK)
@@ -393,8 +394,7 @@
     for b in range(4):
         total = total + contract(blocks[b].astype(F32) * (inverse / lams[b]), blocks[b], LANES)
         spd.append(total)
-    eliminate(spd, [eye] * 4, upper, solved, (lambda: send_near(1),))
-    pass_on(1)
+    eliminate(spd, [eye] * 4, upper, solved, (lambda: None, lambda: None, lambda: pass_on(1)))
     spd, rhs = [], []
     for b in range(4):
         if b == 0:
@@ -405,7 +405,8 @@
             first = contract(low, blocks[b], PLAIN)
             spd.append(contract(first, first, ROWS) * inverse + eye * lams[b])
             rhs.append(contract(first, low, ROWS))
-    eliminate(spd, rhs, upper2, solved2, (send_rows,))
+    send_rows()
+    eliminate(spd, rhs, upper2, solved2)
     wait_rows()
     cols = wides[...].reshape(NT, WIDTH)
     rows_own = row_ref[...].reshape(NT, BLOCK)

time: 51.4 us -> 51 us (level)
  no operation moved by 1% of the time
where the time goes in v5:
time: 51 us; the launch traced here: 50.9 us
  Pallas kernels  47.9 us (94%)
  local copies, waits for them, and re-layouts  1.6 us (3%)
  between operations  1.36 us (3%)
    pallas_call x1, Pallas kernels, factored_tile(): pl.pallas_call(whole_kernel, in_specs=[hbm] * 4 + [pl.BlockSpec(memory_sp...  47.9 us

profile of v5, /device:TPU:1, one launch (start us, length us, event | category | flops | bytes accessed | tf_op | source)
XLA Modules:
  0.0 50.9 jit_solution(28650673467939436)
XLA Ops:
  0.0 0.0 copy-start
  1.3 0.0 copy-done
  1.4 0.8 %constant_dynamic-slice_fusion.table_hbm = s32[3,8192]{1,0:T(4,128)} fusion(s32[3,16384]{1,0:T(4,128)S(1)} %copy-done, s32[]{:T(128)S(6)} %select_n.3), kind=kLoop, calls=%fused_computation | loop fusion | bytes 196612 | tf_op jit(solution)/shard_map/dynamic_slice | solution.py:494
  2.2 47.9 %factored.1 = f32[128,1024]{1,0:T(8,128)S(1)} custom-call(bf16[90,2,1440]{2,1,0:T(2,128)(2,1)} %bitcast.5, bf16[2,720,768]{2,1,0:T(8,128)(2,1)} %constant.6.clone.basis_hbm, bf16[90,8192]{1,0:T(8,128)(2,1)} %leg_hbm.1, s32[3,8192]{1,0:T(4,128)} %constant_dynamic-slice_fusion.table_hbm, f32[1]{0:T(128)S(6)} %copy.10.ridge_ref), custom_call_target="tpu_custom_call" | custom-call | tf_op jit(solution)/shard_map/factored/pallas_call | solution.py:449
  50.1 0.8 %copy.8 = f32[128,1024]{1,0:T(8,128)} copy(f32[128,1024]{1,0:T(8,128)S(1)} %factored.1) | data formatting | bytes 1048576
Async XLA Ops:
  0.0 1.3 %copy-start = (s32[3,16384]{1,0:T(4,128)S(1)}, s32[3,16384]{1,0:T(4,128)}, u32[]{:S(2)}) copy-start(s32[3,16384]{1,0:T(4,128)} %param.8) | copy-start | bytes 589828
